TPU v7x, 32 devices: a whole 2x2x4 slice. The times are simulated.
32 devices in a mesh: groups: 2 (over x), seq: 4 (over y, core), chan: 4 (over z).
Axes of the slice: x: 2, y: 2, z: 4, core: 2. Of those that a mesh axis runs over, the one named last changes fastest.
Arguments:
- dna_act: bfloat16 [6, 2048, 1280], P('groups', 'seq', 'chan'), parts along dimension 0, may hold values from -5 to 5
- conv_weight: bfloat16 [5, 1280, 1536], P(None, 'chan'), may hold values from -0.078125 to 0.078125
- head_weight: bfloat16 [7611, 1536], P(None, 'chan'), may hold values from -0.078125 to 0.078125
- track_ids: int32 [1024], P('groups'), parts along dimension 0, may hold values from 0 to 7610, as said below
- bin_mask: int32 [6, 1024], P('groups', ('seq', 'chan')), parts along dimension 0, may hold values 0 or 1
- counts: int32 [6, 1024, 512], P('groups', ('seq', 'chan')), parts along dimension 0, may hold values from 0 to 3
Outputs:
- grad_input: bfloat16 [6, 2048, 1280], P('groups', 'seq', 'chan'), parts along dimension 0
- grad_conv: float32 [10, 1280, 1536], P('groups', 'chan', 'seq'), parts along dimension 0
- grad_tracks: float32 [1024, 1536], P(('groups', 'seq'), 'chan'), parts along dimension 0
There are 2 independent parts, one for each index of `groups`. A program takes and returns all parts, laid end to end along the dimension named above; an argument that names none is the same for every part. Nothing has to cross between parts.
Inputs may be any that keep to these rules, and one draw needn't show every extreme that they name: `track_ids`: the 512 track numbers are distinct.
All inputs are finite; a program needn't handle non-finite values. No bound on the sum of `bin_mask` on one device may be relied on, other than what follows from the above.
Results may differ from a plain program's by a relative error of at most 0.011.
Values may be sent and summed in bfloat16 or wider, within the bound.
No kernel may reach another device: no remote copies, remote signals or barrier semaphores. Data moves between devices by JAX's collectives and lax.ppermute only.
A program may use at most 128 MiB of HBM per device.

v0:
```python
import jax
import jax.numpy as jnp
from jax import lax
from jax.sharding import PartitionSpec as P

KSIZE = 5


def padded_2(cells, sides, width):
    for axis, dim in sides:
        count = lax.axis_size(axis)
        ends = count - 1
        head = lax.slice_in_dim(cells, 0, width, axis=dim)
        tail = lax.slice_in_dim(cells, cells.shape[dim] - width, cells.shape[dim], axis=dim)
        cells = jnp.concatenate(
            [
                lax.ppermute(tail, axis, [(i, (i + 1) % count) for i in range(ends)]),
                cells,
                lax.ppermute(head, axis, [((i + 1) % count, i) for i in range(ends)]),
            ],
            axis=dim,
        )
    return cells


def exact_gelu(values):
    return jax.nn.gelu(values, approximate=False)


def local(dna_act, conv_weight, head_weight, track_ids, bin_mask, counts):
    seq_count, positions, channels = dna_act.shape
    out_width = conv_weight.shape[2]
    gelu_out, gelu_back = jax.vjp(exact_gelu, dna_act.astype(jnp.float32))
    activated = gelu_out.astype(jnp.bfloat16)
    padded = padded_2(activated, (("seq", 1),), 2)
    windows = jnp.concatenate(
        [padded[:, offset : offset + positions] for offset in range(KSIZE)], axis=2
    )
    flat_weight = conv_weight.reshape(KSIZE * channels, out_width)
    conv_part = jnp.einsum("stj,jo->sto", windows, flat_weight, preferred_element_type=jnp.float32)
    pooled_part = conv_part.reshape(seq_count, positions // 2, 2, out_width).sum(axis=2) * 0.5
    bin_rows = lax.psum_scatter(
        pooled_part.astype(jnp.bfloat16), "chan", scatter_dimension=1, tiled=True
    )
    local_rows = jnp.take(head_weight, track_ids, axis=0)
    chosen = lax.all_gather(local_rows, "chan", axis=1, tiled=True)
    logits = jnp.einsum("snd,md->snm", bin_rows, chosen, preferred_element_type=jnp.float32)
    mask_column = bin_mask.astype(jnp.float32)[:, :, None]
    grad_logit = (mask_column * (jnp.exp(logits) - counts.astype(jnp.float32))).astype(jnp.bfloat16)
    grad_bins = jnp.einsum(
        "snm,md->snd", grad_logit, chosen, preferred_element_type=jnp.float32
    ).astype(jnp.bfloat16)
    slab_grad = lax.all_gather(grad_bins, "chan", axis=1, tiled=True)
    track_part = jnp.einsum("snm,snd->md", grad_logit, bin_rows, preferred_element_type=jnp.float32)
    track_summed = lax.psum_scatter(
        track_part.astype(jnp.bfloat16), "seq", scatter_dimension=0, tiled=True
    )
    grad_tracks = lax.psum_scatter(track_summed, "chan", scatter_dimension=1, tiled=True).astype(
        jnp.float32
    )
    rim_grad = padded_2(slab_grad, (("seq", 1),), 1)
    wide_grad = jnp.repeat(rim_grad, 2, axis=1) * 0.5
    projected = jnp.einsum(
        "sqo,jo->sqj", wide_grad, flat_weight, preferred_element_type=jnp.float32
    )
    projected = projected.reshape(seq_count, positions + 4, KSIZE, channels)
    grad_acts = projected[:, 4 : 4 + positions, 0]
    for offset in range(1, KSIZE):
        grad_acts = grad_acts + projected[:, 4 - offset : 4 - offset + positions, offset]
    grad_input = gelu_back(grad_acts)[0].astype(jnp.bfloat16)
    slab_upsampled = jnp.repeat(slab_grad, 2, axis=1) * 0.5
    flat_grad = jnp.einsum(
        "stj,sto->jo", windows, slab_upsampled, preferred_element_type=jnp.float32
    )
    grad_conv = lax.psum_scatter(
        flat_grad.reshape(KSIZE, channels, out_width).astype(jnp.bfloat16),
        "seq",
        scatter_dimension=2,
        tiled=True,
    ).astype(jnp.float32)
    return (grad_input, grad_conv, grad_tracks)


def solution(mesh):
    in_specs = (
        P("groups", "seq", "chan"),
        P(None, "chan", None),
        P(None, "chan"),
        P("groups"),
        P("groups", ("seq", "chan")),
        P("groups", ("seq", "chan"), None),
    )
    out_specs = (
        P("groups", "seq", "chan"),
        P("groups", "chan", "seq"),
        P(("groups", "seq"), "chan"),
    )
    return jax.shard_map(local, mesh=mesh, in_specs=in_specs, out_specs=out_specs, check_vma=False)
```

profile of v0, /device:TPU:0, one launch (start us, length us, event | category | flops | bytes accessed | tf_op | source)
XLA Modules:
  0.0 317.8 jit_solution(13602244970949401829)
XLA Ops:
  7.2 1.7 copy.17
  8.9 6.0 %fusion.12 = (bf16[3,512,320]{2,1,0:T(8,128)(2,1)S(1)}, f32[3,512,320]{2,1,0:T(8,128)}) fusion(bf16[3,512,320]{2,1,0:T(8,128)(2,1)S(1)} %copy.17), kind=kLoop, calls=%fused_computation.19 | loop fusion | flops 32440320 | bytes 3932160 | tf_op jit(solution)/shard_map/convert_element_type | solution.py:34
  15.0 2.4 collective-permute-start
  17.4 1.3 collective-permute-start.1
  18.7 5.2 %gather_fusion = bf16[512,384]{1,0:T(8,128)(2,1)S(1)} fusion(bf16[7611,384]{1,0:T(8,128)(2,1)} %param.8, s32[1024]{0:T(1024)S(1)} %pad_clamp_fusion), kind=kCustom, calls=%fused_computation | custom fusion | bytes 788480 | tf_op jit(solution)/shard_map/jit(_take)/gather | solution.py:45
  23.9 0.9 broadcast_select_fusion
  24.9 0.0 reduce-scatter.9.cloned.1.call-start
  24.9 3.4 %pad_maximum_fusion = (bf16[3,512,320]{2,1,0:T(8,128)(2,1)S(1)}, bf16[3,512,320]{2,1,0:T(8,128)(2,1)}, bf16[3,512,320]{2,1,0:T(8,128)(2,1)}, bf16[3,512,320]{2,1,0:T(8,128)(2,1)}) fusion(bf16[3,2,320]{2,1,0:T(2,128)(2,1)S(1)} %collective-permute-done.1, bf16[3,512,320]{2,1,0:T(8,128)(2,1)S(1)} %get-tuple-element.12, ...), kind=kLoop, calls=%fused_computation.71 | loop fusion | flops 7864320 | bytes 4922880 | tf_op jit(solution)/shard_map/concatenate | solution.py:15
  28.3 9.0 %concatenate.17 = bf16[3,512,1600]{2,1,0:T(8,128)(2,1)} concatenate(bf16[3,512,320]{2,1,0:T(8,128)(2,1)} %get-tuple-element.20, bf16[3,512,320]{2,1,0:T(8,128)(2,1)} %get-tuple-element.21, bf16[3,512,320]{2,1,0:T(8,128)(2,1)S(1)} %get-tuple-element.12, bf16[3,512,320]{2,1,0:T(8,128)(2,1)} %get-tuple-element.17, bf16[3,512,320]{2,1,0:T(8,128)(2,1)S(1)} %get-tuple-element.16), dimensions={2} | concatenate | bytes 9830400 | tf_op jit(solution)/shard_map/concatenate | solution.py:36
  37.3 11.0 %dot_general.24 = bf16[3,256,2,1600]{3,2,1,0:T(2,128)(2,1)} reshape(bf16[3,512,1600]{2,1,0:T(8,128)(2,1)} %concatenate.17) | data formatting | bytes 9830400 | tf_op jit(solution)/shard_map/stj,jo->sto/dot_general | solution.py:40
  48.3 12.4 %fusion.7 = f32[3,256,1536]{2,1,0:T(8,128)S(1)} fusion(bf16[1600,1536,1,1]{1,0,3,2:T(8,128)(2,1)} %bitcast.55, bf16[3,256,2,1600]{3,2,1,0:T(2,128)(2,1)} %dot_general.24), kind=kOutput, calls=%fused_computation.14 | convolution fusion | flops 7550926848 | bytes 14548992 | tf_op jit(solution)/shard_map/stj,jo->sto/dot_general | solution.py:40
  60.7 2.1 multiply_convert_fusion
  62.8 0.0 reduce-scatter.11.cloned.1.call-start
  62.9 0.6 copy-done.4
  63.5 2.7 all-gather.3.cloned.1.call-done
  66.2 49.4 %reduce-scatter.9.cloned.1.call-done = bf16[3,64,1536]{2,1,0:T(8,128)(2,1)} async-done(((bf16[3,256,1536]{2,1,0:T(8,128)(2,1)}), bf16[3,64,1536]{2,1,0:T(8,128)(2,1)}) %reduce-scatter.9.cloned.1.call-update) | async-done | bytes 589840 | tf_op jit(solution)/shard_map/reduce_scatter | solution.py:42
  115.6 2.3 fusion.62
  117.9 1.8 fusion.6
  119.7 0.0 all-gather.5.cloned.1.call-start
  119.8 2.7 convolution_convert_fusion
  122.5 0.2 reduce-scatter.15.cloned.1.call-start
  122.7 7.8 %copy.19 = bf16[1600,3,512]{2,0,1:T(8,128)(2,1)} copy(bf16[1600,3,512]{0,2,1:T(8,128)(2,1)} %bitcast.49) | data formatting | bytes 9830400 | tf_op jit(solution)/shard_map/stj,sto->jo/dot_general | solution.py:72
  130.5 16.8 %reduce-scatter.11.cloned.1.call-done = bf16[128,1536]{1,0:T(8,128)(2,1)} async-done(((bf16[512,1536]{1,0:T(8,128)(2,1)}), bf16[128,1536]{1,0:T(8,128)(2,1)}) %reduce-scatter.11.cloned.1.call-update) | async-done | bytes 393232 | tf_op jit(solution)/shard_map/reduce_scatter | solution.py:55
  147.3 1.9 copy.26
  149.2 0.0 reduce-scatter.13.cloned.1.call-start
  149.3 50.0 %all-gather.5.cloned.1.call-done = bf16[3,256,1536]{2,1,0:T(8,128)(2,1)} async-done(((bf16[3,64,1536]{2,1,0:T(8,128)(2,1)}), bf16[3,256,1536]{2,1,0:T(8,128)(2,1)}) %all-gather.5.cloned.1.call-update) | async-done | bytes 2359312 | tf_op jit(solution)/shard_map/all_gather | solution.py:53
  199.3 1.9 broadcast_multiply_fusion
  201.2 4.0 %broadcast_in_dim.23 = bf16[3,256,2,1536]{3,2,1,0:T(2,128)(2,1)} broadcast(bf16[3,256,1536]{2,1,0:T(8,128)(2,1)S(1)} %broadcast_multiply_fusion), dimensions={0,1,3} | broadcast | bytes 7077888 | tf_op jit(solution)/shard_map/broadcast_in_dim | solution.py:71
  205.2 10.7 %reshape.44 = bf16[3,512,1536,1]{2,1,0,3:T(8,128)(2,1)} reshape(bf16[3,256,2,1536]{3,2,1,0:T(2,128)(2,1)} %broadcast_in_dim.23) | data formatting | bytes 9437184 | tf_op jit(solution)/shard_map/mul | solution.py:71
  215.9 12.5 %bitcast_convert_fusion = bf16[5,320,1536]{2,1,0:T(8,128)(2,1)} fusion(bf16[5,320,3,512]{3,1,0,2:T(8,128)(2,1)} %bitcast.52, bf16[3,512,1536,1]{2,1,0,3:T(8,128)(2,1)} %reshape.44), kind=kOutput, calls=%fused_computation.1 | convolution fusion | flops 7552204800 | bytes 14548992 | tf_op jit(solution)/shard_map/stj,sto->jo/dot_general | solution.py:72
  228.5 11.7 %copy.24 = bf16[5,320,1536]{1,0,2:T(8,128)(2,1)} copy(bf16[5,320,1536]{2,1,0:T(8,128)(2,1)} %bitcast_convert_fusion) | data formatting | bytes 9830400
  240.2 12.8 %reshape.49 = bf16[1536,1600]{1,0:T(8,128)(2,1)} reshape(bf16[1536,5,320]{2,1,0:T(8,128)(2,1)} %bitcast.50) | data formatting | bytes 9830400
  253.0 1.0 fusion.66
  254.0 1.6 collective-permute-start.2
  255.5 1.3 collective-permute-start.3
  256.9 3.2 collective-permute-done.3
  260.0 3.2 %maximum_multiply_fusion = bf16[3,258,1536]{2,1,0:T(8,128)(2,1)S(1)} fusion(bf16[3,1,1536]{2,1,0:T(2,128)(2,1)S(1)} %collective-permute-done.3, bf16[3,256,1536]{2,1,0:T(8,128)(2,1)} %all-gather.5.cloned.1.call-done, bf16[3,1,1536]{2,1,0:T(2,128)(2,1)S(1)} %collective-permute-done.2), kind=kLoop, calls=%fused_computation.18 | loop fusion | flops 9510912 | bytes 4755456 | tf_op jit(solution)/shard_map/mul | solution.py:62
  263.2 4.3 %broadcast_in_dim.22 = bf16[3,258,2,1536]{3,2,1,0:T(2,128)(2,1)} broadcast(bf16[3,258,1536]{2,1,0:T(8,128)(2,1)S(1)} %maximum_multiply_fusion), dimensions={0,1,3} | broadcast | bytes 7133184 | tf_op jit(solution)/shard_map/broadcast_in_dim | solution.py:62
  267.5 6.4 %reshape.42 = bf16[3,516,1536,1]{2,1,0,3:T(8,128)(2,1)} reshape(bf16[3,258,2,1536]{3,2,1,0:T(2,128)(2,1)} %broadcast_in_dim.22) | data formatting | bytes 9510912 | tf_op jit(solution)/shard_map/mul | solution.py:62
  273.9 14.4 %fusion.2 = f32[3,516,5,320]{3,1,2,0:T(8,128)S(1)} fusion(bf16[5,320,1536]{2,1,0:T(8,128)(2,1)} %param.7, bf16[3,516,1536,1]{2,1,0,3:T(8,128)(2,1)} %reshape.42), kind=kOutput, calls=%fused_computation.4 | convolution fusion | flops 7608729600 | bytes 19577856 | tf_op jit(solution)/shard_map/sqo,jo->sqj/dot_general | solution.py:63
  288.4 2.1 fusion.18
  290.5 1.4 copy.20
  291.9 1.0 copy.27
  292.9 0.7 convert_element_type.47
  293.6 8.8 %reduce-scatter.13.cloned.1.call-done = bf16[384,1600]{1,0:T(8,128)(2,1)} async-done(((bf16[1536,1600]{1,0:T(8,128)(2,1)}), bf16[384,1600]{1,0:T(8,128)(2,1)}) %reduce-scatter.13.cloned.1.call-update) | async-done | bytes 1228816
  302.4 3.3 %reshape.50 = bf16[384,5,320]{2,1,0:T(8,128)(2,1)S(1)} reshape(bf16[384,1600]{1,0:T(8,128)(2,1)} %reduce-scatter.13.cloned.1.call-done) | data formatting | bytes 2457600
  305.6 2.4 copy.25
  308.0 2.9 convert_element_type.45
  (25 shorter events, 0.2 us)
Async XLA Ops:
  7.2 59.0 %all-gather.3.cloned.1.call-start = ((), (), s32[]{:S(2)}) async-start(), calls=%async_computation.5 | async-start | bytes 1966080 | tf_op jit(solution)/shard_map/all_gather | solution.py:46
  8.9 9.8 %copy-start.3 = (s32[512]{0:T(512)S(1)}, s32[512]{0:T(512)}, u32[]{:S(2)}) copy-start(s32[512]{0:T(512)} %param.9) | copy-start | bytes 6148
  15.0 10.0 %collective-permute-start = (bf16[3,2,320]{2,1,0:T(2,128)(2,1)S(1)}, bf16[3,2,320]{2,1,0:T(2,128)(2,1)S(1)}, u32[]{:S(2)}, u32[]{:S(2)}) collective-permute-start(bf16[3,2,320]{2,1,0:T(2,128)(2,1)S(1)} %get-tuple-element.23), channel_id=1, source_target_pairs={{0,4},{4,8},{8,12},{1,5},{5,9},{9,13},{2,6},{6,10},{10,14},{3,7},{... | collective-permute-start | bytes 11528 | tf_op jit(solution)/shard_map/ppermute | solution.py:17
  17.4 7.6 %collective-permute-start.1 = (bf16[3,2,320]{2,1,0:T(2,128)(2,1)S(1)}, bf16[3,2,320]{2,1,0:T(2,128)(2,1)S(1)}, u32[]{:S(2)}, u32[]{:S(2)}) collective-permute-start(bf16[3,2,320]{2,1,0:T(2,128)(2,1)S(1)} %get-tuple-element.22), channel_id=1, source_target_pairs={{4,0},{8,4},{12,8},{5,1},{9,5},{13,9},{6,2},{10,6},{14,10},{7,3},{... | collective-permute-start | bytes 11528 | tf_op jit(solution)/shard_map/ppermute | solution.py:19
  24.9 90.7 %reduce-scatter.9.cloned.1.call-start = ((), (), s32[]{:S(2)}) async-start(), calls=%async_computation.4 | async-start | bytes 2949120 | tf_op jit(solution)/shard_map/reduce_scatter | solution.py:42
  62.8 0.7 copy-start.4
  62.8 52.8 %copy-start.2 = (s32[3,64,512]{2,1,0:T(8,128)S(1)}, s32[3,64,512]{2,1,0:T(8,128)}, u32[]{:S(2)}) copy-start(s32[3,64,512]{2,1,0:T(8,128)} %param.11) | copy-start | bytes 1179652
  62.8 84.5 %reduce-scatter.11.cloned.1.call-start = ((), (), s32[]{:S(2)}) async-start(), calls=%async_computation.7 | async-start | bytes 1966080 | tf_op jit(solution)/shard_map/reduce_scatter | solution.py:55
  115.6 2.3 copy-start.1
  119.7 79.6 %all-gather.5.cloned.1.call-start = ((), (), s32[]{:S(2)}) async-start(), calls=%async_computation.6 | async-start | bytes 2949120 | tf_op jit(solution)/shard_map/all_gather | solution.py:53
  122.5 169.4 %reduce-scatter.15.cloned.1.call-start = ((), (), s32[]{:S(2)}) async-start(), calls=%async_computation.9 | async-start | bytes 491520
  149.2 153.1 %reduce-scatter.13.cloned.1.call-start = ((), (), s32[]{:S(2)}) async-start(), calls=%async_computation.8 | async-start | bytes 6389760
  254.0 2.9 collective-permute-start.2
  255.5 4.5 %collective-permute-start.3 = (bf16[3,1,1536]{2,1,0:T(2,128)(2,1)S(1)}, bf16[3,1,1536]{2,1,0:T(2,128)(2,1)S(1)}, u32[]{:S(2)}, u32[]{:S(2)}) collective-permute-start(bf16[3,1,1536]{2,1,0:T(2,128)(2,1)S(1)} %get-tuple-element.15), channel_id=1, source_target_pairs={{4,0},{8,4},{12,8},{5,1},{9,5},{13,9},{6,2},{10,6},{14,10},{7,3},{... | collective-permute-start | bytes 27656 | tf_op jit(solution)/shard_map/ppermute | solution.py:19
  273.9 14.4 %copy-start = (f32[3,512,320]{2,1,0:T(8,128)S(1)}, f32[3,512,320]{2,1,0:T(8,128)}, u32[]{:S(2)}) copy-start(f32[3,512,320]{2,1,0:T(8,128)} %get-tuple-element.13) | copy-start | bytes 5898244
Sparse Core Ops, SparseCore 0:
  25.0 41.1 all-gather.2
  68.5 47.0 reduce-scatter.8
  119.8 27.4 reduce-scatter.10
  149.3 49.9 all-gather.4
  201.4 19.4 reduce-scatter.14
  253.1 49.2 reduce-scatter.12
where the time goes:
time: 320 us; the launch traced here: 318 us
  waiting for transfers between devices  131 us (41%)
  local copies, waits for them, and re-layouts  96.2 us (30%)
  matrix products  46.1 us (14%)
  other arithmetic  23.2 us (7%)
  between operations  14.3 us (4%)
  starting transfers between devices  6.99 us (2%)
    all_gather x1, waiting for transfers between devices, local(): slab_grad = lax.all_gather(grad_bins, 'chan', axis=1, tiled=True)  50 us
    reduce_scatter x1, waiting for transfers between devices, local(): lax.psum_scatter(pooled_part.astype(jnp.bfloat16), 'chan', scatter_dimens...  49.4 us
    unnamed x18, local copies, waits for them, and re-layouts  36.8 us
    reduce_scatter x1, waiting for transfers between devices, local(): lax.psum_scatter(track_part.astype(jnp.bfloat16), 'seq', scatter_dimensio...  16.8 us
    dot_general x1, matrix products, local(): jnp.einsum('sqo,jo->sqj', wide_grad, flat_weight, preferred_element_type=...  14.4 us
    dot_general x1, matrix products, local(): jnp.einsum('stj,sto->jo', windows, slab_upsampled, preferred_element_type...  12.5 us
    dot_general x1, matrix products, local(): jnp.einsum('stj,jo->sto', windows, flat_weight, preferred_element_type=jn...  12.4 us
    dot_general x1, local copies, waits for them, and re-layouts, local(): jnp.einsum('stj,jo->sto', windows, flat_weight, preferred_element_type=jn...  11 us
  transfers between devices with their start and end apart: 10, of which 6 were waited for; matrix products, arithmetic and copies ran while one was open for 46% of the time, Pallas kernels for 0%

commit v1 on v0

--- a/solution.py
+++ b/solution.py
@@ -4,6 +4,28 @@
 from jax.sharding import PartitionSpec as P
 
 KSIZE = 5
+
+
+def joined_along(pieces, dim):
+    pieces = jnp.moveaxis(pieces, 0, dim)
+    lengths = pieces.shape
+    return pieces.reshape(*lengths[:dim], lengths[dim] * lengths[dim + 1], *lengths[dim + 2 :])
+
+
+def gather_around(value, axis, dim):
+    size = lax.axis_size(axis)
+    pairs = [(i, (i + 1) % size) for i in range(size)]
+    back = [(b, a) for a, b in pairs]
+    lower, upper = ([], [])
+    for step in range(size - 1):
+        if step % 2 == 0:
+            lower.append(lax.ppermute(lower[-1] if lower else value, axis, pairs))
+        else:
+            upper.append(lax.ppermute(upper[-1] if upper else value, axis, back))
+    parts = jnp.stack([*lower[::-1], value, *upper])
+    shift = lax.axis_index(axis) - len(lower)
+    parts = parts[(jnp.arange(size) - shift) % size]
+    return joined_along(parts, dim)
 
 
 def padded_2(cells, sides, width):
@@ -50,7 +72,7 @@
     grad_bins = jnp.einsum(
         "snm,md->snd", grad_logit, chosen, preferred_element_type=jnp.float32
     ).astype(jnp.bfloat16)
-    slab_grad = lax.all_gather(grad_bins, "chan", axis=1, tiled=True)
+    slab_grad = gather_around(grad_bins, "chan", 1)
     track_part = jnp.einsum("snm,snd->md", grad_logit, bin_rows, preferred_element_type=jnp.float32)
     track_summed = lax.psum_scatter(
         track_part.astype(jnp.bfloat16), "seq", scatter_dimension=0, tiled=True

time: 320 us -> 287 us (0.90)
  waiting for transfers between devices: 131 us -> 95.3 us
  starting transfers between devices: 6.99 us -> 11 us
    all_gather x1 -> x0, waiting for transfers between devices: 50 us -> none  [local(): slab_grad = lax.all_gather(grad_bins, 'chan', axis=1, tiled=True)]
    ppermute x0 -> x3, waiting for transfers between devices: none -> 30.1 us  [the longest x2 27.4 us: gather_around(): lower.append(lax.ppermute(lower[-1] if lower else value, axis, pairs))]
    reduce_scatter x1, waiting for transfers between devices: 16.8 us -> 0.01 us  [local(): lax.psum_scatter(track_part.astype(jnp.bfloat16), 'seq', scatter_dimensio...]
    ppermute x0 -> x3, starting transfers between devices: none -> 3.88 us  [the longest x1 3 us: gather_around(): upper.append(lax.ppermute(upper[-1] if upper else value, axis, back))]
    unnamed x8 -> x7, waiting for transfers between devices: 8.85 us -> 11.4 us
    unnamed x18 -> x26, local copies, waits for them, and re-layouts: 36.8 us -> 36.8 us
  transfers between devices with their start and end apart: 10 -> 12, of which waited for: 6 -> 7; matrix products, arithmetic and copies ran while one was open for 46% -> 50% of each run, Pallas kernels for 0% -> 0%
where the time goes in v1:
time: 287 us; the launch traced here: 285 us
  local copies, waits for them, and re-layouts  99.3 us (35%)
  waiting for transfers between devices  95.3 us (33%)
  matrix products  44.5 us (16%)
  other arithmetic  21.1 us (7%)
  between operations  14 us (5%)
  starting transfers between devices  11 us (4%)
    reduce_scatter x1, waiting for transfers between devices, local(): lax.psum_scatter(pooled_part.astype(jnp.bfloat16), 'chan', scatter_dimens...  49.4 us
    unnamed x26, local copies, waits for them, and re-layouts  36.8 us
    ppermute x2, waiting for transfers between devices, gather_around(): lower.append(lax.ppermute(lower[-1] if lower else value, axis, pairs))  27.4 us
    dot_general x1, matrix products, local(): jnp.einsum('sqo,jo->sqj', wide_grad, flat_weight, preferred_element_type=...  14.9 us
    dot_general x1, matrix products, local(): jnp.einsum('stj,sto->jo', windows, slab_upsampled, preferred_element_type...  12.6 us
    dot_general x1, matrix products, local(): jnp.einsum('stj,jo->sto', windows, flat_weight, preferred_element_type=jn...  12.4 us
    unnamed x7, waiting for transfers between devices  11.4 us
    dot_general x1, local copies, waits for them, and re-layouts, local(): jnp.einsum('stj,jo->sto', windows, flat_weight, preferred_element_type=jn...  10.9 us
  transfers between devices with their start and end apart: 12, of which 7 were waited for; matrix products, arithmetic and copies ran while one was open for 50% of the time, Pallas kernels for 0%

profile of v1, /device:TPU:0, one launch (start us, length us, event | category | flops | bytes accessed | tf_op | source)
XLA Modules:
  0.0 285.2 jit_solution(9246368447598740054)
XLA Ops:
  7.2 1.7 copy.18
  8.9 6.0 %fusion.12 = (bf16[3,512,320]{2,1,0:T(8,128)(2,1)S(1)}, f32[3,512,320]{2,1,0:T(8,128)}) fusion(bf16[3,512,320]{2,1,0:T(8,128)(2,1)S(1)} %copy.18), kind=kLoop, calls=%fused_computation.20 | loop fusion | flops 32440320 | bytes 3932160 | tf_op jit(solution)/shard_map/convert_element_type | solution.py:56
  15.0 1.3 collective-permute-start.1
  16.3 3.0 %collective-permute-start = (bf16[3,2,320]{2,1,0:T(2,128)(2,1)S(1)}, bf16[3,2,320]{2,1,0:T(2,128)(2,1)S(1)}, u32[]{:S(2)}, u32[]{:S(2)}) collective-permute-start(bf16[3,2,320]{2,1,0:T(2,128)(2,1)S(1)} %get-tuple-element.23), channel_id=1, source_target_pairs={{0,4},{4,8},{8,12},{1,5},{5,9},{9,13},{2,6},{6,10},{10,14},{3,7},{... | collective-permute-start | bytes 11528 | tf_op jit(solution)/shard_map/ppermute | solution.py:39
  19.3 5.2 %gather_fusion = bf16[512,384]{1,0:T(8,128)(2,1)S(1)} fusion(bf16[7611,384]{1,0:T(8,128)(2,1)} %param.8, s32[1024]{0:T(1024)S(1)} %pad_clamp_fusion.1), kind=kCustom, calls=%fused_computation | custom fusion | bytes 788480 | tf_op jit(solution)/shard_map/jit(_take)/gather | solution.py:67
  24.6 0.9 broadcast_select_fusion
  25.6 3.4 %pad_maximum_fusion.1 = (bf16[3,512,320]{2,1,0:T(8,128)(2,1)S(1)}, bf16[3,512,320]{2,1,0:T(8,128)(2,1)}, bf16[3,512,320]{2,1,0:T(8,128)(2,1)}, bf16[3,512,320]{2,1,0:T(8,128)(2,1)}) fusion(bf16[3,2,320]{2,1,0:T(2,128)(2,1)S(1)} %collective-permute-done.1, bf16[3,512,320]{2,1,0:T(8,128)(2,1)S(1)} %get-tuple-element.12, ...), kind=kLoop, calls=%fused_computation.73 | loop fusion | flops 7864320 | bytes 4922880 | tf_op jit(solution)/shard_map/concatenate | solution.py:37
  28.9 9.0 %concatenate.17 = bf16[3,512,1600]{2,1,0:T(8,128)(2,1)} concatenate(bf16[3,512,320]{2,1,0:T(8,128)(2,1)} %get-tuple-element.20, bf16[3,512,320]{2,1,0:T(8,128)(2,1)} %get-tuple-element.21, bf16[3,512,320]{2,1,0:T(8,128)(2,1)S(1)} %get-tuple-element.12, bf16[3,512,320]{2,1,0:T(8,128)(2,1)} %get-tuple-element.17, bf16[3,512,320]{2,1,0:T(8,128)(2,1)S(1)} %get-tuple-element.16), dimensions={2} | concatenate | bytes 9830400 | tf_op jit(solution)/shard_map/concatenate | solution.py:58
  37.9 10.9 %dot_general.24 = bf16[3,256,2,1600]{3,2,1,0:T(2,128)(2,1)} reshape(bf16[3,512,1600]{2,1,0:T(8,128)(2,1)} %concatenate.17) | data formatting | bytes 9830400 | tf_op jit(solution)/shard_map/stj,jo->sto/dot_general | solution.py:62
  48.8 12.4 %fusion.7 = f32[3,256,1536]{2,1,0:T(8,128)S(1)} fusion(bf16[1600,1536,1,1]{1,0,3,2:T(8,128)(2,1)} %bitcast.70, bf16[3,256,2,1600]{3,2,1,0:T(2,128)(2,1)} %dot_general.24), kind=kOutput, calls=%fused_computation.15 | convolution fusion | flops 7550926848 | bytes 14548992 | tf_op jit(solution)/shard_map/stj,jo->sto/dot_general | solution.py:62
  61.2 2.0 multiply_convert_fusion
  63.3 0.6 copy-done.8
  63.9 1.0 all-gather.2.cloned.1.call-done
  65.0 49.4 %reduce-scatter.9.cloned.1.call-done = bf16[3,64,1536]{2,1,0:T(8,128)(2,1)} async-done(((bf16[3,256,1536]{2,1,0:T(8,128)(2,1)}), bf16[3,64,1536]{2,1,0:T(8,128)(2,1)}) %reduce-scatter.9.cloned.1.call-update) | async-done | bytes 589840 | tf_op jit(solution)/shard_map/reduce_scatter | solution.py:64
  114.3 2.3 fusion.62
  116.7 1.8 fusion.6
  118.6 0.5 convolution_convert_fusion
  119.1 0.9 collective-permute-start.2
  119.9 3.0 %collective-permute-start.4 = (bf16[3,64,1536]{2,1,0:T(8,128)(2,1)S(1)}, bf16[3,64,1536]{2,1,0:T(8,128)(2,1)S(1)}, u32[]{:S(2)}, u32[]{:S(2)}) collective-permute-start(bf16[3,64,1536]{2,1,0:T(8,128)(2,1)S(1)} %convolution_convert_fusion), channel_id=1, source_target_pairs={{1,0},{2,1},{3,2},{0,3},{5,4},{6,5},{7,6},{4,7},{9,8},{10,9},{11,1... | collective-permute-start | bytes 1769480 | tf_op jit(solution)/shard_map/ppermute | solution.py:24
  122.9 14.2 %collective-permute-done.2 = bf16[3,64,1536]{2,1,0:T(8,128)(2,1)S(1)} collective-permute-done((bf16[3,64,1536]{2,1,0:T(8,128)(2,1)S(1)}, bf16[3,64,1536]{2,1,0:T(8,128)(2,1)S(1)}, u32[]{:S(2)}, u32[]{:S(2)}) %collective-permute-start.2) | collective-permute-done | bytes 589856 | tf_op jit(solution)/shard_map/ppermute | solution.py:22
  137.2 7.9 %copy.21 = bf16[1600,3,512]{2,0,1:T(8,128)(2,1)} copy(bf16[1600,3,512]{0,2,1:T(8,128)(2,1)} %bitcast.58) | data formatting | bytes 9830400 | tf_op jit(solution)/shard_map/stj,sto->jo/dot_general | solution.py:94
  145.1 2.7 collective-permute-done.4
  147.8 13.2 %collective-permute-done.3 = bf16[3,64,1536]{2,1,0:T(8,128)(2,1)} collective-permute-done((bf16[3,64,1536]{2,1,0:T(8,128)(2,1)S(1)}, bf16[3,64,1536]{2,1,0:T(8,128)(2,1)}, u32[]{:S(2)}, u32[]{:S(2)}) %collective-permute-start.3) | collective-permute-done | bytes 589856 | tf_op jit(solution)/shard_map/ppermute | solution.py:22
  161.0 1.9 pad_maximum_fusion
  162.9 2.1 gather_fusion.1
  165.0 1.9 copy.20
  166.9 0.4 broadcast_multiply_fusion
  167.3 4.0 %broadcast_in_dim.24 = bf16[3,256,2,1536]{3,2,1,0:T(2,128)(2,1)} broadcast(bf16[3,256,1536]{2,1,0:T(8,128)(2,1)S(1)} %broadcast_multiply_fusion), dimensions={0,1,3} | broadcast | bytes 7077888 | tf_op jit(solution)/shard_map/broadcast_in_dim | solution.py:93
  171.3 10.7 %reshape.105 = bf16[3,512,1536,1]{2,1,0,3:T(8,128)(2,1)} reshape(bf16[3,256,2,1536]{3,2,1,0:T(2,128)(2,1)} %broadcast_in_dim.24) | data formatting | bytes 9437184 | tf_op jit(solution)/shard_map/mul | solution.py:93
  182.0 1.9 copy.28
  184.0 12.6 %bitcast_convert_fusion = bf16[5,320,1536]{2,1,0:T(8,128)(2,1)} fusion(bf16[5,320,3,512]{3,1,0,2:T(8,128)(2,1)} %bitcast.64, bf16[3,512,1536,1]{2,1,0,3:T(8,128)(2,1)} %reshape.105), kind=kOutput, calls=%fused_computation.2 | convolution fusion | flops 7552204800 | bytes 14548992 | tf_op jit(solution)/shard_map/stj,sto->jo/dot_general | solution.py:94
  196.5 11.7 %copy.26 = bf16[5,320,1536]{1,0,2:T(8,128)(2,1)} copy(bf16[5,320,1536]{2,1,0:T(8,128)(2,1)} %bitcast_convert_fusion) | data formatting | bytes 9830400
  208.3 12.8 %reshape.110 = bf16[1536,1600]{1,0:T(8,128)(2,1)} reshape(bf16[1536,5,320]{2,1,0:T(8,128)(2,1)} %bitcast.59) | data formatting | bytes 9830400
  221.1 1.3 collective-permute-start.5
  222.4 1.3 collective-permute-start.6
  223.7 3.5 %collective-permute-done.6 = bf16[3,1,1536]{2,1,0:T(2,128)(2,1)S(1)} collective-permute-done((bf16[3,1,1536]{2,1,0:T(2,128)(2,1)S(1)}, bf16[3,1,1536]{2,1,0:T(2,128)(2,1)S(1)}, u32[]{:S(2)}, u32[]{:S(2)}) %collective-permute-start.6) | collective-permute-done | bytes 9248 | tf_op jit(solution)/shard_map/ppermute | solution.py:41
  227.2 0.8 maximum_multiply_fusion
  228.0 4.3 %broadcast_in_dim.23 = bf16[3,258,2,1536]{3,2,1,0:T(2,128)(2,1)} broadcast(bf16[3,258,1536]{2,1,0:T(8,128)(2,1)S(1)} %maximum_multiply_fusion), dimensions={0,1,3} | broadcast | bytes 7133184 | tf_op jit(solution)/shard_map/broadcast_in_dim | solution.py:84
  232.2 6.3 %reshape.103 = bf16[3,516,1536,1]{2,1,0,3:T(8,128)(2,1)} reshape(bf16[3,258,2,1536]{3,2,1,0:T(2,128)(2,1)} %broadcast_in_dim.23) | data formatting | bytes 9510912 | tf_op jit(solution)/shard_map/mul | solution.py:84
  238.6 14.9 %fusion.2 = f32[3,516,5,320]{3,1,2,0:T(8,128)S(1)} fusion(bf16[5,320,1536]{2,1,0:T(8,128)(2,1)} %param.7, bf16[3,516,1536,1]{2,1,0,3:T(8,128)(2,1)} %reshape.103), kind=kOutput, calls=%fused_computation.5 | convolution fusion | flops 7608729600 | bytes 19577856 | tf_op jit(solution)/shard_map/sqo,jo->sqj/dot_general | solution.py:85
  253.6 2.1 fusion.18
  255.7 1.4 copy.22
  257.1 1.0 copy.29
  258.1 0.7 convert_element_type.47
  258.8 11.3 %reduce-scatter.13.cloned.1.call-done = bf16[384,1600]{1,0:T(8,128)(2,1)} async-done(((bf16[1536,1600]{1,0:T(8,128)(2,1)}), bf16[384,1600]{1,0:T(8,128)(2,1)}) %reduce-scatter.13.cloned.1.call-update) | async-done | bytes 1228816
  270.1 3.3 %reshape.111 = bf16[384,5,320]{2,1,0:T(8,128)(2,1)S(1)} reshape(bf16[384,1600]{1,0:T(8,128)(2,1)} %reduce-scatter.13.cloned.1.call-done) | data formatting | bytes 2457600
  273.3 2.4 copy.27
  275.8 2.9 %convert_element_type.45 = f32[5,320,384]{2,1,0:T(8,128)} convert(bf16[5,320,384]{2,1,0:T(8,128)(2,1)} %copy.27) | non-fusion elementwise | flops 614400 | bytes 3686400 | tf_op jit(solution)/shard_map/convert_element_type | solution.py:102
  (41 shorter events, 0.4 us)
Async XLA Ops:
  7.2 57.8 %all-gather.2.cloned.1.call-start = ((), (), s32[]{:S(2)}) async-start(), calls=%async_computation.5 | async-start | bytes 1966080 | tf_op jit(solution)/shard_map/all_gather | solution.py:68
  8.9 10.4 %copy-start.7 = (s32[512]{0:T(512)S(1)}, s32[512]{0:T(512)}, u32[]{:S(2)}) copy-start(s32[512]{0:T(512)} %param.9) | copy-start | bytes 6148
  15.0 10.6 %collective-permute-start.1 = (bf16[3,2,320]{2,1,0:T(2,128)(2,1)S(1)}, bf16[3,2,320]{2,1,0:T(2,128)(2,1)S(1)}, u32[]{:S(2)}, u32[]{:S(2)}) collective-permute-start(bf16[3,2,320]{2,1,0:T(2,128)(2,1)S(1)} %get-tuple-element.22), channel_id=1, source_target_pairs={{4,0},{8,4},{12,8},{5,1},{9,5},{13,9},{6,2},{10,6},{14,10},{7,3},{... | collective-permute-start | bytes 11528 | tf_op jit(solution)/shard_map/ppermute | solution.py:41
  16.3 9.3 %collective-permute-start = (bf16[3,2,320]{2,1,0:T(2,128)(2,1)S(1)}, bf16[3,2,320]{2,1,0:T(2,128)(2,1)S(1)}, u32[]{:S(2)}, u32[]{:S(2)}) collective-permute-start(bf16[3,2,320]{2,1,0:T(2,128)(2,1)S(1)} %get-tuple-element.23), channel_id=1, source_target_pairs={{0,4},{4,8},{8,12},{1,5},{5,9},{9,13},{2,6},{6,10},{10,14},{3,7},{... | collective-permute-start | bytes 11528 | tf_op jit(solution)/shard_map/ppermute | solution.py:39
  25.5 88.9 %reduce-scatter.9.cloned.1.call-start = ((), (), s32[]{:S(2)}) async-start(), calls=%async_computation.4 | async-start | bytes 2949120 | tf_op jit(solution)/shard_map/reduce_scatter | solution.py:64
  63.3 0.7 copy-start.8
  63.3 51.1 %copy-start.6 = (s32[3,64,512]{2,1,0:T(8,128)S(1)}, s32[3,64,512]{2,1,0:T(8,128)}, u32[]{:S(2)}) copy-start(s32[3,64,512]{2,1,0:T(8,128)} %param.11) | copy-start | bytes 1179652
  63.3 118.7 %reduce-scatter.11.cloned.1.call-start = ((), (), s32[]{:S(2)}) async-start(), calls=%async_computation.6 | async-start | bytes 1966080 | tf_op jit(solution)/shard_map/reduce_scatter | solution.py:77
  114.3 2.3 copy-start.5
  116.7 1.8 copy-start.1
  118.5 138.6 %reduce-scatter.15.cloned.1.call-start = ((), (), s32[]{:S(2)}) async-start(), calls=%async_computation.8 | async-start | bytes 491520
  119.0 26.1 %copy-start.2 = (bf16[3,64,1536]{2,1,0:T(8,128)(2,1)}, bf16[3,64,1536]{2,1,0:T(8,128)(2,1)S(1)}, u32[]{:S(2)}) copy-start(bf16[3,64,1536]{2,1,0:T(8,128)(2,1)S(1)} %convolution_convert_fusion) | copy-start | bytes 1769476
  119.1 18.1 %collective-permute-start.2 = (bf16[3,64,1536]{2,1,0:T(8,128)(2,1)S(1)}, bf16[3,64,1536]{2,1,0:T(8,128)(2,1)S(1)}, u32[]{:S(2)}, u32[]{:S(2)}) collective-permute-start(bf16[3,64,1536]{2,1,0:T(8,128)(2,1)S(1)} %convolution_convert_fusion), channel_id=1, source_target_pairs={{0,1},{1,2},{2,3},{3,0},{4,5},{5,6},{6,7},{7,4},{8,9},{9,10},{10,1... | collective-permute-start | bytes 1769480 | tf_op jit(solution)/shard_map/ppermute | solution.py:22
  119.9 27.9 %collective-permute-start.4 = (bf16[3,64,1536]{2,1,0:T(8,128)(2,1)S(1)}, bf16[3,64,1536]{2,1,0:T(8,128)(2,1)S(1)}, u32[]{:S(2)}, u32[]{:S(2)}) collective-permute-start(bf16[3,64,1536]{2,1,0:T(8,128)(2,1)S(1)} %convolution_convert_fusion), channel_id=1, source_target_pairs={{1,0},{2,1},{3,2},{0,3},{5,4},{6,5},{7,6},{4,7},{9,8},{10,9},{11,1... | collective-permute-start | bytes 1769480 | tf_op jit(solution)/shard_map/ppermute | solution.py:24
  137.2 8.0 %copy-start.3 = (bf16[3,64,1536]{2,1,0:T(8,128)(2,1)}, bf16[3,64,1536]{2,1,0:T(8,128)(2,1)S(1)}, u32[]{:S(2)}) copy-start(bf16[3,64,1536]{2,1,0:T(8,128)(2,1)S(1)} %collective-permute-done.2) | copy-start | bytes 1769476
  137.2 23.8 %collective-permute-start.3 = (bf16[3,64,1536]{2,1,0:T(8,128)(2,1)S(1)}, bf16[3,64,1536]{2,1,0:T(8,128)(2,1)}, u32[]{:S(2)}, u32[]{:S(2)}) collective-permute-start(bf16[3,64,1536]{2,1,0:T(8,128)(2,1)S(1)} %collective-permute-done.2), channel_id=1, source_target_pairs={{0,1},{1,2},{2,3},{3,0},{4,5},{5,6},{6,7},{7,4},{8,9},{9,10},{10,1... | collective-permute-start | bytes 1769480 | tf_op jit(solution)/shard_map/ppermute | solution.py:22
  147.8 13.2 %copy-start.4 = (bf16[3,64,1536]{2,1,0:T(8,128)(2,1)}, bf16[3,64,1536]{2,1,0:T(8,128)(2,1)S(1)}, u32[]{:S(2)}) copy-start(bf16[3,64,1536]{2,1,0:T(8,128)(2,1)S(1)} %collective-permute-done.4) | copy-start | bytes 1769476
  183.9 86.2 %reduce-scatter.13.cloned.1.call-start = ((), (), s32[]{:S(2)}) async-start(), calls=%async_computation.7 | async-start | bytes 6389760
  221.1 2.6 collective-permute-start.5
  222.4 4.8 %collective-permute-start.6 = (bf16[3,1,1536]{2,1,0:T(2,128)(2,1)S(1)}, bf16[3,1,1536]{2,1,0:T(2,128)(2,1)S(1)}, u32[]{:S(2)}, u32[]{:S(2)}) collective-permute-start(bf16[3,1,1536]{2,1,0:T(2,128)(2,1)S(1)} %get-tuple-element.15), channel_id=1, source_target_pairs={{4,0},{8,4},{12,8},{5,1},{9,5},{13,9},{6,2},{10,6},{14,10},{7,3},{... | collective-permute-start | bytes 27656 | tf_op jit(solution)/shard_map/ppermute | solution.py:41
  238.6 14.9 %copy-start = (f32[3,512,320]{2,1,0:T(8,128)S(1)}, f32[3,512,320]{2,1,0:T(8,128)}, u32[]{:S(2)}) copy-start(f32[3,512,320]{2,1,0:T(8,128)} %get-tuple-element.13) | copy-start | bytes 5898244
Sparse Core Ops, SparseCore 0:
  25.6 39.3 all-gather.1
  67.3 47.0 reduce-scatter.8
  118.6 27.4 reduce-scatter.10
  184.0 19.0 reduce-scatter.14
  221.2 48.8 reduce-scatter.12
